TPU v7x, 256 devices: a whole 4x4x8 slice. The times are simulated.
256 devices in a mesh: comp: 4 (over z_lo), dom: 64 (over y, x, z_hi, core).
Axes of the slice: x: 4, y: 4, z: 8 (z_hi: 2, z_lo: 4; z = z_hi * 4 + z_lo), core: 2. Of those that a mesh axis runs over, the one named last changes fastest.
Arguments:
- airside_exchange: bfloat16 [4, 4, 65536], P('comp', None, 'dom'), may hold values from -6 to 6
- regrid_matrix_partitions: bfloat16 [4, 512, 4, 128, 128], P('comp', 'dom'), may hold values from -0.25 to 0.25
- regrid_destination_latitude: int32 [4, 512, 4], P('comp', 'dom'), may hold values from 0 to 2047, all different within a row
- thermal_departure: float32 [32, 2048, 128], P(None, ('comp', 'dom')), may hold values from -6 to 6
- diffusivity_coefficient: float32 [31, 2048, 128], P(None, ('comp', 'dom')), may hold values from 0.05 to 3
- elevation_anomaly_profile: float32 [2048, 128], P(('comp', 'dom')), may hold values from -3 to 3
- depth_integrated_volume_flow: float32 [2, 2048, 128], P(None, ('comp', 'dom')), may hold values from -2 to 2
- marine_indicator: int32 [2048, 128], P(('comp', 'dom')), may hold values 0 or 1
Outputs:
- ocean_temperature: float32 [32, 2048, 128], P(None, ('comp', 'dom'))
- ocean_height: float32 [2048, 128], P(('comp', 'dom'))
- atm_surface: bfloat16 [4, 2, 65536], P('comp', None, 'dom')
Inputs may be any that keep to these rules, and one draw needn't show every extreme that they name: `regrid_destination_latitude`: each (section, source block) names 4 different ocean blocks, and every ocean block is named somewhere; ocean block b is grid row b.
All inputs are finite; a program needn't handle non-finite values. No bound on the sum of `marine_indicator` on one device may be relied on, other than what follows from the above.
Results may differ from a plain program's by a relative error of at most 0.0048.
Values may be sent and summed in bfloat16 or wider, within the bound.
No kernel may reach another device: no remote copies, remote signals or barrier semaphores. Data moves between devices by JAX's collectives and lax.ppermute only.
A program may use at most 64 MiB of HBM per device.

v0:
```python
import jax
import jax.numpy as jnp
from jax import lax
from jax.sharding import PartitionSpec as P

NSTEP = 2
NSUB = 8
wave_gain = 0.35
stress_gain = 0.1
fresh_gain = 0.1
spread_gain = 0.2
heating_gain = 0.5


def with_halo(block, sides, width):
    for axis, dim in sides:
        count = lax.axis_size(axis)
        forward = [(i, i + 1) for i in range(count - 1)]
        backward = [(target, source) for source, target in forward]
        low = lax.ppermute(
            lax.slice_in_dim(block, block.shape[dim] - width, None, axis=dim), axis, forward
        )
        high = lax.ppermute(lax.slice_in_dim(block, 0, width, axis=dim), axis, backward)
        block = jnp.concatenate([low, block, high], axis=dim)
    return block


def vertical_solve(explicit, diffusivity_coefficient):
    levels_all = explicit.shape[0]
    solved = []
    ratios = []
    for layer_index in range(levels_all):
        upward = (
            diffusivity_coefficient[layer_index - 1]
            if layer_index > 0
            else jnp.zeros_like(explicit[0])
        )
        downward = (
            diffusivity_coefficient[layer_index]
            if layer_index < levels_all - 1
            else jnp.zeros_like(explicit[0])
        )
        pivots = 1.0 + upward + downward
        if layer_index > 0:
            pivots = pivots - upward * ratios[-1]
            solved.append((explicit[layer_index] + upward * solved[-1]) / pivots)
        else:
            solved.append(explicit[layer_index] / pivots)
        ratios.append(downward / pivots)
    result = [solved[-1]]
    for layer_index in range(levels_all - 2, -1, -1):
        result.append(solved[layer_index] + ratios[layer_index] * result[-1])
    return jnp.stack(result[::-1])


def shards(
    airside_exchange,
    regrid_matrix_partitions,
    regrid_destination_latitude,
    thermal_departure,
    diffusivity_coefficient,
    elevation_anomaly_profile,
    depth_integrated_volume_flow,
    marine_indicator,
):
    groups = lax.axis_size("comp")
    blocks_dom = lax.axis_size("dom")
    rows_here = elevation_anomaly_profile.shape[0]
    width_row = elevation_anomaly_profile.shape[1]
    fields = airside_exchange.shape[1]
    source_blocks = regrid_matrix_partitions.shape[1]
    links = regrid_matrix_partitions.shape[2]
    block_cols = regrid_matrix_partitions.shape[3]
    all_rows = groups * blocks_dom * rows_here
    sources = airside_exchange[0].reshape(fields, source_blocks, block_cols)
    weights = regrid_matrix_partitions[0]
    partial_terms = jnp.einsum(
        "fsa,skab->skfb", sources, weights, preferred_element_type=jnp.float32
    )
    partial_terms = partial_terms.reshape(source_blocks * links, fields, width_row)
    targets = regrid_destination_latitude[0].reshape(-1)
    owner_group = targets // (blocks_dom * rows_here)
    owner_block = targets // rows_here % blocks_dom
    inside_row = targets % rows_here
    placed = owner_block * (groups * rows_here) + owner_group * rows_here + inside_row
    dense_terms = (
        jnp.zeros((all_rows, fields, width_row), jnp.float32).at[placed].add(partial_terms)
    )
    block_sums = lax.psum_scatter(dense_terms, "dom", scatter_dimension=0, tiled=True)
    ocean_flux = lax.psum_scatter(block_sums, "comp", scatter_dimension=0, tiled=True)
    heating = ocean_flux[:, 0, :]
    freshwater = ocean_flux[:, 1, :]
    stress_east = ocean_flux[:, 2, :]
    stress_north = ocean_flux[:, 3, :]
    wet = marine_indicator.astype(jnp.float32)
    face_east = wet * jnp.roll(wet, -1, axis=1)
    height = elevation_anomaly_profile
    flow_east = depth_integrated_volume_flow[0]
    flow_north = depth_integrated_volume_flow[1]
    advected_quantity = thermal_departure
    face_north = None
    for outer_step in range(NSTEP):
        for substep in range(NSUB):
            extended = with_halo(
                jnp.stack([height, flow_north, wet, stress_north]), ((("comp", "dom"), 1),), 1
            )
            edge_height = extended[0]
            edge_north = extended[1]
            edge_wet = extended[2]
            edge_stress = extended[3]
            face_north = edge_wet[:-1] * edge_wet[1:]
            new_east = face_east * (
                flow_east
                - wave_gain * (jnp.roll(height, -1, axis=1) - height)
                + stress_gain * stress_east
            )
            north_rows = face_north * (
                edge_north[:-1]
                - wave_gain * (edge_height[1:] - edge_height[:-1])
                + stress_gain * edge_stress[:-1]
            )
            height = (
                height
                - wave_gain
                * (new_east - jnp.roll(new_east, 1, axis=1) + north_rows[1:] - north_rows[:-1])
                + fresh_gain * freshwater * wet
            )
            flow_east = new_east
            flow_north = north_rows[1:]
        edge_tracer = with_halo(advected_quantity, ((("comp", "dom"), 1),), 1)
        along_east = face_east * (jnp.roll(advected_quantity, -1, axis=2) - advected_quantity)
        along_north = face_north * (edge_tracer[:, 1:] - edge_tracer[:, :-1])
        laplace = (
            along_east - jnp.roll(along_east, 1, axis=2) + along_north[:, 1:] - along_north[:, :-1]
        )
        explicit = advected_quantity + spread_gain * laplace
        explicit = explicit.at[0].add(heating_gain * heating * wet)
        advected_quantity = vertical_solve(explicit, diffusivity_coefficient)
    surface = jnp.stack([advected_quantity[0], height]).astype(jnp.bfloat16)
    shard_rows = lax.all_gather(surface, ("comp", "dom"), axis=1, tiled=True)
    count_rows = shard_rows.shape[1]
    selector = (targets[:, None] == jnp.arange(count_rows, dtype=jnp.int32)[None, :]).astype(
        jnp.bfloat16
    )
    picked = jnp.einsum("nr,frb->nfb", selector, shard_rows, preferred_element_type=jnp.float32)
    chosen = picked.astype(jnp.bfloat16).reshape(source_blocks, links, 2, width_row)
    returned = jnp.einsum("skfb,skab->fsa", chosen, weights, preferred_element_type=jnp.float32)
    return (
        advected_quantity,
        height,
        returned.reshape(1, 2, source_blocks * block_cols).astype(jnp.bfloat16),
    )


def solution(mesh):
    return jax.shard_map(
        shards,
        mesh=mesh,
        in_specs=(
            P("comp", None, "dom"),
            P("comp", "dom", None, None, None),
            P("comp", "dom", None),
            P(None, ("comp", "dom"), None),
            P(None, ("comp", "dom"), None),
            P(("comp", "dom"), None),
            P(None, ("comp", "dom"), None),
            P(("comp", "dom"), None),
        ),
        out_specs=(
            P(None, ("comp", "dom"), None),
            P(("comp", "dom"), None),
            P("comp", None, "dom"),
        ),
        check_vma=False,
    )
```

profile of v0, /device:TPU:1, one launch (start us, length us, event | category | flops | bytes accessed | tf_op | source)
XLA Modules:
  0.0 1094.7 jit_solution(4753517972119351040)
XLA Ops:
  11.7 3.6 scatter_fusion
  15.3 4.5 copy.18
  20.7 5.1 collective-permute-start.16
  25.9 7.0 collective-permute-start.17
  33.1 404.4 %reduce-scatter.3.cloned.1.call-done = f32[32,4,128]{2,0,1:T(8,128)} async-done(((f32[2048,4,128]{2,0,1:T(8,128)}), f32[32,4,128]{2,0,1:T(8,128)}) %reduce-scatter.3.cloned.1.call-update) | async-done | bytes 65552 | tf_op jit(solution)/shard_map/reduce_scatter | solution.py:89
  437.7 26.5 %reduce-scatter.5.cloned.1.call-done = f32[8,4,128]{2,0,1:T(8,128)} async-done(((f32[32,4,128]{2,0,1:T(8,128)}), f32[8,4,128]{2,0,1:T(8,128)}) %reduce-scatter.5.cloned.1.call-update) | async-done | bytes 16400 | tf_op jit(solution)/shard_map/reduce_scatter | solution.py:90
  465.0 7.5 collective-permute-start
  475.5 5.8 collective-permute-done.1
  484.2 2.4 collective-permute-start.3
  487.4 5.6 collective-permute-done.3
  495.1 2.4 collective-permute-start.5
  498.4 5.6 collective-permute-done.5
  506.1 2.4 collective-permute-start.7
  509.4 6.5 collective-permute-done.7
  518.0 2.4 collective-permute-start.9
  521.2 6.5 collective-permute-done.9
  529.9 2.4 collective-permute-start.11
  533.1 6.5 collective-permute-done.11
  541.8 2.4 collective-permute-start.13
  545.0 6.5 collective-permute-done.13
  553.7 2.4 collective-permute-start.15
  556.9 6.5 collective-permute-done.15
  571.4 8.0 collective-permute-start.35
  579.6 2.4 collective-permute-start.20
  584.1 7.6 collective-permute-done.21
  596.5 7.2 collective-permute-done.23
  608.3 7.2 collective-permute-done.25
  620.2 7.2 collective-permute-done.27
  632.1 7.2 collective-permute-done.29
  644.0 7.2 collective-permute-done.31
  655.9 7.6 collective-permute-done.33
  665.6 420.0 %all-gather.2.cloned.1.call-done = bf16[2,2048,128]{2,1,0:T(8,128)(2,1)} async-done(((bf16[2,8,128]{2,1,0:T(8,128)(2,1)}), bf16[2,2048,128]{2,1,0:T(8,128)(2,1)}) %all-gather.2.cloned.1.call-update) | async-done | bytes 1048592 | tf_op jit(solution)/shard_map/all_gather | solution.py:140
  (301 shorter events, 73.4 us)
Async XLA Ops:
  7.2 430.3 %reduce-scatter.3.cloned.1.call-start = ((), (), s32[]{:S(2)}) async-start(), calls=%async_computation.2 | async-start | bytes 4259840 | tf_op jit(solution)/shard_map/reduce_scatter | solution.py:89
  19.9 444.3 %reduce-scatter.5.cloned.1.call-start = ((), (), s32[]{:S(2)}) async-start(), calls=%async_computation.3 | async-start | bytes 81920 | tf_op jit(solution)/shard_map/reduce_scatter | solution.py:90
  20.7 542.7 %collective-permute-start.16 = (f32[32,1,128]{2,1,0:T(1,128)S(1)}, f32[32,1,128]{2,1,0:T(1,128)S(1)}, u32[]{:S(2)}, u32[]{:S(2)}) collective-permute-start(f32[32,1,128]{2,1,0:T(1,128)S(1)} %get-tuple-element.179), channel_id=1, source_target_pairs={{1,0},{2,1},{3,2},{4,3},{5,4},{6,5},{7,6},{8,7},{9,8},{10,9},{11,1... | collective-permute-start | bytes 49160 | tf_op jit(solution)/shard_map/ppermute | solution.py:23
  25.9 537.6 %collective-permute-start.17 = (f32[32,1,128]{2,1,0:T(1,128)S(1)}, f32[32,1,128]{2,1,0:T(1,128)S(1)}, u32[]{:S(2)}, u32[]{:S(2)}) collective-permute-start(f32[32,1,128]{2,1,0:T(1,128)S(1)} %get-tuple-element.178), channel_id=1, source_target_pairs={{0,1},{1,2},{2,3},{3,4},{4,5},{5,6},{6,7},{7,8},{8,9},{9,10},{10,1... | collective-permute-start | bytes 49160 | tf_op jit(solution)/shard_map/ppermute | solution.py:20
  437.5 648.2 %all-gather.2.cloned.1.call-start = ((), (), s32[]{:S(2)}) async-start(), calls=%async_computation.4 | async-start | bytes 1052672 | tf_op jit(solution)/shard_map/all_gather | solution.py:140
  465.0 10.5 collective-permute-start
  472.5 8.8 collective-permute-start.1
  482.2 5.2 collective-permute-start.2
  484.2 8.8 collective-permute-start.3
  493.2 5.2 collective-permute-start.4
  495.1 8.8 collective-permute-start.5
  504.2 5.2 collective-permute-start.6
  506.1 9.7 collective-permute-start.7
  516.1 5.2 collective-permute-start.8
  518.0 9.7 collective-permute-start.9
  528.0 5.2 collective-permute-start.10
  529.9 9.7 collective-permute-start.11
  539.8 5.2 collective-permute-start.12
  541.8 9.7 collective-permute-start.13
  551.7 5.2 collective-permute-start.14
  553.7 9.7 collective-permute-start.15
  564.7 14.6 %collective-permute-start.18 = (f32[4,1,128]{2,1,0:T(1,128)S(1)}, f32[4,1,128]{2,1,0:T(1,128)S(1)}, u32[]{:S(2)}, u32[]{:S(2)}) collective-permute-start(f32[4,1,128]{2,1,0:T(1,128)S(1)} %get-tuple-element.211), channel_id=1, source_target_pairs={{0,1},{1,2},{2,3},{3,4},{4,5},{5,6},{6,7},{7,8},{8,9},{9,10},{10,1... | collective-permute-start | bytes 6152 | tf_op jit(solution)/shard_map/ppermute | solution.py:20
  566.7 12.7 %collective-permute-start.19 = (f32[4,1,128]{2,1,0:T(1,128)S(1)}, f32[4,1,128]{2,1,0:T(1,128)S(1)}, u32[]{:S(2)}, u32[]{:S(2)}) collective-permute-start(f32[4,1,128]{2,1,0:T(1,128)S(1)} %get-tuple-element.210), channel_id=1, source_target_pairs={{1,0},{2,1},{3,2},{4,3},{5,4},{6,5},{7,6},{8,7},{9,8},{10,9},{11,1... | collective-permute-start | bytes 6152 | tf_op jit(solution)/shard_map/ppermute | solution.py:23
  569.4 94.7 %collective-permute-start.34 = (f32[32,1,128]{2,1,0:T(1,128)S(1)}, f32[32,1,128]{2,1,0:T(1,128)S(1)}, u32[]{:S(2)}, u32[]{:S(2)}) collective-permute-start(f32[32,1,128]{2,1,0:T(1,128)S(1)} %get-tuple-element.177), channel_id=1, source_target_pairs={{1,0},{2,1},{3,2},{4,3},{5,4},{6,5},{7,6},{8,7},{9,8},{10,9},{11,1... | collective-permute-start | bytes 49160 | tf_op jit(solution)/shard_map/ppermute | solution.py:23
  571.4 92.8 %collective-permute-start.35 = (f32[32,1,128]{2,1,0:T(1,128)S(1)}, f32[32,1,128]{2,1,0:T(1,128)S(1)}, u32[]{:S(2)}, u32[]{:S(2)}) collective-permute-start(f32[32,1,128]{2,1,0:T(1,128)S(1)} %get-tuple-element.176), channel_id=1, source_target_pairs={{0,1},{1,2},{2,3},{3,4},{4,5},{5,6},{6,7},{7,8},{8,9},{9,10},{10,1... | collective-permute-start | bytes 49160 | tf_op jit(solution)/shard_map/ppermute | solution.py:20
  582.0 9.7 collective-permute-start.21
  593.9 9.7 collective-permute-start.23
  605.8 9.7 collective-permute-start.25
  617.7 9.7 collective-permute-start.27
  629.6 9.7 collective-permute-start.29
  641.4 9.7 collective-permute-start.31
  653.3 10.1 collective-permute-start.33
  (15 other events, 1948.1 us)
Sparse Core Ops, SparseCore 0:
  20.0 417.4 reduce-scatter.2
  439.9 24.2 reduce-scatter.4
  665.3 420.2 all-gather.1
where the time goes:
time: 1100 us; the launch traced here: 1090 us
  waiting for transfers between devices  952 us (87%)
  starting transfers between devices  96.4 us (9%)
  other arithmetic  15.4 us (1%)
  between operations  15 us (1%)
  local copies, waits for them, and re-layouts  12.8 us (1%)
    all_gather x1, waiting for transfers between devices, shards(): shard_rows = lax.all_gather(surface, ('comp', 'dom'), axis=1, tiled=True)  420 us
    reduce_scatter x1, waiting for transfers between devices, shards(): lax.psum_scatter(dense_terms, 'dom', scatter_dimension=0, tiled=True)  404 us
    ppermute x18, waiting for transfers between devices, with_halo(): lax.ppermute(lax.slice_in_dim(block, 0, width, axis=dim), axis, backward)  101 us
    ppermute x18, starting transfers between devices, with_halo(): lax.ppermute(lax.slice_in_dim(block, block.shape[dim] - width, None, axis...  52.3 us
    ppermute x18, starting transfers between devices, with_halo(): lax.ppermute(lax.slice_in_dim(block, 0, width, axis=dim), axis, backward)  44.1 us
    reduce_scatter x1, waiting for transfers between devices, shards(): lax.psum_scatter(block_sums, 'comp', scatter_dimension=0, tiled=True)  26.5 us
  transfers between devices with their start and end apart: 39, of which 18 were waited for; matrix products, arithmetic and copies ran while one was open for 1% of the time, Pallas kernels for 0%

commit v1 on v0

--- a/solution.py
+++ b/solution.py
@@ -10,6 +10,11 @@
 fresh_gain = 0.1
 spread_gain = 0.2
 heating_gain = 0.5
+
+
+def gather_over(x, name, dim):
+    outgoing = jnp.stack([x] * lax.axis_size(name))
+    return jnp.concatenate(lax.all_to_all(outgoing, name, 0, 0), axis=dim)
 
 
 def with_halo(block, sides, width):
@@ -137,7 +142,7 @@
         explicit = explicit.at[0].add(heating_gain * heating * wet)
         advected_quantity = vertical_solve(explicit, diffusivity_coefficient)
     surface = jnp.stack([advected_quantity[0], height]).astype(jnp.bfloat16)
-    shard_rows = lax.all_gather(surface, ("comp", "dom"), axis=1, tiled=True)
+    shard_rows = gather_over(surface, ("comp", "dom"), 1)
     count_rows = shard_rows.shape[1]
     selector = (targets[:, None] == jnp.arange(count_rows, dtype=jnp.int32)[None, :]).astype(
         jnp.bfloat16

time: 1100 us -> 1160 us (1.055)
  starting transfers between devices: 96.4 us -> 145 us
  waiting for transfers between devices: 952 us -> 975 us
    unnamed x3 -> x4, waiting for transfers between devices: 0.05 us -> 838 us
    reduce_scatter x2 -> x0, waiting for transfers between devices: 431 us -> none  [the longest x1 404 us: shards(): lax.psum_scatter(dense_terms, 'dom', scatter_dimension=0, tiled=True)]
    all_gather x1 -> x0, waiting for transfers between devices: 420 us -> none  [shards(): shard_rows = lax.all_gather(surface, ('comp', 'dom'), axis=1, tiled=True)]
    all_to_all x0 -> x1, starting transfers between devices: none -> 49 us  [gather_over(): return jnp.concatenate(lax.all_to_all(outgoing, name, 0, 0), axis=dim)]
    all_to_all x0 -> x1, waiting for transfers between devices: none -> 30.6 us  [gather_over(): return jnp.concatenate(lax.all_to_all(outgoing, name, 0, 0), axis=dim)]
where the time goes in v1:
time: 1160 us
  waiting for transfers between devices  975 us (84%)
  starting transfers between devices  145 us (12%)
  between operations  16.7 us (1%)
    unnamed x4, waiting for transfers between devices  838 us
    ppermute x18, waiting for transfers between devices, with_halo(): lax.ppermute(lax.slice_in_dim(block, 0, width, axis=dim), axis, backward)  106 us
    ppermute x18, starting transfers between devices, with_halo(): lax.ppermute(lax.slice_in_dim(block, block.shape[dim] - width, None, axis...  52 us
    all_to_all x1, starting transfers between devices, gather_over(): return jnp.concatenate(lax.all_to_all(outgoing, name, 0, 0), axis=dim)  49 us
    ppermute x18, starting transfers between devices, with_halo(): lax.ppermute(lax.slice_in_dim(block, 0, width, axis=dim), axis, backward)  44.1 us
    all_to_all x1, waiting for transfers between devices, gather_over(): return jnp.concatenate(lax.all_to_all(outgoing, name, 0, 0), axis=dim)  30.6 us
  transfers between devices with their start and end apart: 39, of which 18 were waited for; matrix products, arithmetic and copies ran while one was open for 1% of the time, Pallas kernels for 0%

profile of v1, /device:TPU:1, one launch (start us, length us, event | category | flops | bytes accessed | tf_op | source)
XLA Modules:
  0.0 1158.8 jit_solution(3629796743667284304)
XLA Ops:
  11.7 3.6 scatter_fusion
  15.4 5.1 collective-permute-start.16
  20.6 7.0 collective-permute-start.17
  28.9 790.8 %all-reduce.5.cloned.1.call-done = f32[2048,4,128]{2,1,0:T(4,128)} async-done(((f32[2048,4,128]{2,1,0:T(4,128)}), f32[2048,4,128]{2,1,0:T(4,128)}) %all-reduce.5.cloned.1.call-update) | async-done | bytes 4194320
  822.8 47.2 %all-reduce.7.cloned.1.call-done = f32[32,4,128]{2,1,0:T(4,128)} async-done(((f32[32,4,128]{2,1,0:T(4,128)}), f32[32,4,128]{2,1,0:T(4,128)}) %all-reduce.7.cloned.1.call-update) | async-done | bytes 65552
  870.9 7.2 collective-permute-start
  880.4 6.5 collective-permute-done.1
  889.1 2.4 collective-permute-start.3
  891.7 6.3 collective-permute-done.3
  900.1 2.4 collective-permute-start.5
  902.6 6.3 collective-permute-done.5
  911.1 2.4 collective-permute-start.7
  913.7 7.2 collective-permute-done.7
  923.0 2.4 collective-permute-start.9
  925.5 7.2 collective-permute-done.9
  934.9 2.4 collective-permute-start.11
  937.4 7.2 collective-permute-done.11
  946.8 2.4 collective-permute-start.13
  949.3 7.2 collective-permute-done.13
  958.6 2.4 collective-permute-start.15
  961.2 7.2 collective-permute-done.15
  976.3 8.0 collective-permute-start.35
  984.6 2.4 collective-permute-start.20
  989.1 7.6 collective-permute-done.21
  1001.4 7.2 collective-permute-done.23
  1013.3 7.2 collective-permute-done.25
  1025.2 7.2 collective-permute-done.27
  1037.1 7.2 collective-permute-done.29
  1048.9 7.2 collective-permute-done.31
  1060.8 7.6 collective-permute-done.33
  1070.7 49.0 %all-to-all-start = ((bf16[256,2,8,128]{3,2,1,0:T(8,128)(2,1)}), bf16[256,2,8,128]{3,2,1,0:T(8,128)(2,1)S(1)}, u32[]{:S(2)}, u32[]{:S(2)}) async-start(bf16[256,2,8,128]{3,2,1,0:T(8,128)(2,1)} %stack.158), calls=%async_computation | async-start | bytes 2097152 | tf_op jit(solution)/shard_map/all_to_all | solution.py:17
  1120.1 30.6 %all-to-all-done = bf16[256,2,8,128]{3,2,1,0:T(8,128)(2,1)S(1)} async-done(((bf16[256,2,8,128]{3,2,1,0:T(8,128)(2,1)}), bf16[256,2,8,128]{3,2,1,0:T(8,128)(2,1)S(1)}, u32[]{:S(2)}, u32[]{:S(2)}) %all-to-all-start) | async-done | bytes 1048608 | tf_op jit(solution)/shard_map/all_to_all | solution.py:17
  (305 shorter events, 68.5 us)
Async XLA Ops:
  7.2 812.5 %all-reduce.5.cloned.1.call-start = ((), (), s32[]{:S(2)}) async-start(), calls=%async_computation.1 | async-start | bytes 8388608
  15.4 854.6 %all-reduce.7.cloned.1.call-start = ((), (), s32[]{:S(2)}) async-start(), calls=%async_computation.2 | async-start | bytes 131072
  15.4 952.9 %collective-permute-start.16 = (f32[32,1,128]{2,1,0:T(1,128)S(1)}, f32[32,1,128]{2,1,0:T(1,128)S(1)}, u32[]{:S(2)}, u32[]{:S(2)}) collective-permute-start(f32[32,1,128]{2,1,0:T(1,128)S(1)} %get-tuple-element.179), channel_id=1, source_target_pairs={{1,0},{2,1},{3,2},{4,3},{5,4},{6,5},{7,6},{8,7},{9,8},{10,9},{11,1... | collective-permute-start | bytes 49160 | tf_op jit(solution)/shard_map/ppermute | solution.py:28
  20.6 947.8 %collective-permute-start.17 = (f32[32,1,128]{2,1,0:T(1,128)S(1)}, f32[32,1,128]{2,1,0:T(1,128)S(1)}, u32[]{:S(2)}, u32[]{:S(2)}) collective-permute-start(f32[32,1,128]{2,1,0:T(1,128)S(1)} %get-tuple-element.178), channel_id=1, source_target_pairs={{0,1},{1,2},{2,3},{3,4},{4,5},{5,6},{6,7},{7,8},{8,9},{9,10},{10,1... | collective-permute-start | bytes 49160 | tf_op jit(solution)/shard_map/ppermute | solution.py:25
  870.9 9.5 collective-permute-start
  878.1 8.8 collective-permute-start.1
  887.2 4.5 collective-permute-start.2
  889.1 8.8 collective-permute-start.3
  898.1 4.5 collective-permute-start.4
  900.1 8.8 collective-permute-start.5
  909.2 4.5 collective-permute-start.6
  911.1 9.7 collective-permute-start.7
  921.0 4.5 collective-permute-start.8
  923.0 9.7 collective-permute-start.9
  932.9 4.5 collective-permute-start.10
  934.9 9.7 collective-permute-start.11
  944.8 4.5 collective-permute-start.12
  946.8 9.7 collective-permute-start.13
  958.6 9.7 collective-permute-start.15
  969.7 14.6 %collective-permute-start.18 = (f32[4,1,128]{2,1,0:T(1,128)S(1)}, f32[4,1,128]{2,1,0:T(1,128)S(1)}, u32[]{:S(2)}, u32[]{:S(2)}) collective-permute-start(f32[4,1,128]{2,1,0:T(1,128)S(1)} %get-tuple-element.215), channel_id=1, source_target_pairs={{0,1},{1,2},{2,3},{3,4},{4,5},{5,6},{6,7},{7,8},{8,9},{9,10},{10,1... | collective-permute-start | bytes 6152 | tf_op jit(solution)/shard_map/ppermute | solution.py:25
  971.7 12.7 %collective-permute-start.19 = (f32[4,1,128]{2,1,0:T(1,128)S(1)}, f32[4,1,128]{2,1,0:T(1,128)S(1)}, u32[]{:S(2)}, u32[]{:S(2)}) collective-permute-start(f32[4,1,128]{2,1,0:T(1,128)S(1)} %get-tuple-element.214), channel_id=1, source_target_pairs={{1,0},{2,1},{3,2},{4,3},{5,4},{6,5},{7,6},{8,7},{9,8},{10,9},{11,1... | collective-permute-start | bytes 6152 | tf_op jit(solution)/shard_map/ppermute | solution.py:28
  974.4 94.7 %collective-permute-start.34 = (f32[32,1,128]{2,1,0:T(1,128)S(1)}, f32[32,1,128]{2,1,0:T(1,128)S(1)}, u32[]{:S(2)}, u32[]{:S(2)}) collective-permute-start(f32[32,1,128]{2,1,0:T(1,128)S(1)} %get-tuple-element.177), channel_id=1, source_target_pairs={{1,0},{2,1},{3,2},{4,3},{5,4},{6,5},{7,6},{8,7},{9,8},{10,9},{11,1... | collective-permute-start | bytes 49160 | tf_op jit(solution)/shard_map/ppermute | solution.py:28
  976.3 92.8 %collective-permute-start.35 = (f32[32,1,128]{2,1,0:T(1,128)S(1)}, f32[32,1,128]{2,1,0:T(1,128)S(1)}, u32[]{:S(2)}, u32[]{:S(2)}) collective-permute-start(f32[32,1,128]{2,1,0:T(1,128)S(1)} %get-tuple-element.176), channel_id=1, source_target_pairs={{0,1},{1,2},{2,3},{3,4},{4,5},{5,6},{6,7},{7,8},{8,9},{9,10},{10,1... | collective-permute-start | bytes 49160 | tf_op jit(solution)/shard_map/ppermute | solution.py:25
  984.6 4.5 collective-permute-start.20
  987.0 9.7 collective-permute-start.21
  998.9 9.7 collective-permute-start.23
  1010.8 9.7 collective-permute-start.25
  1022.6 9.7 collective-permute-start.27
  1034.5 9.7 collective-permute-start.29
  1046.4 9.7 collective-permute-start.31
  1058.3 10.1 collective-permute-start.33
  1070.7 80.0 %all-to-all-start = ((bf16[256,2,8,128]{3,2,1,0:T(8,128)(2,1)}), bf16[256,2,8,128]{3,2,1,0:T(8,128)(2,1)S(1)}, u32[]{:S(2)}, u32[]{:S(2)}) async-start(bf16[256,2,8,128]{3,2,1,0:T(8,128)(2,1)} %stack.158), calls=%async_computation | async-start | bytes 2097152 | tf_op jit(solution)/shard_map/all_to_all | solution.py:17
  (16 other events, 4291.4 us)
Sparse Core Ops, SparseCore 0:
  15.5 804.1 all-reduce.4
  822.9 47.0 all-reduce.6
